TPU v7x, 32 devices: a whole 2x2x4 slice. The times are simulated.
32 devices in a mesh: regions: 2 (over y), gz: 8 (over z, x), gy: 2 (over core).
Axes of the slice: x: 2, y: 2, z: 4, core: 2. Of those that a mesh axis runs over, the one named last changes fastest.
Arguments:
- iterate: float32 [16, 32, 128, 256], P(None, ('regions', 'gz'), 'gy'), parts along dimension 1, may hold values from -6 to 6
- residual: float32 [16, 32, 128, 256], P(None, ('regions', 'gz'), 'gy'), parts along dimension 1, may hold values from -16 to 16
- labels: int32 [32, 128, 256], P(('regions', 'gz'), 'gy'), parts along dimension 0, may hold values from 0 to 7
- boundary: int32 [32, 128, 256], P(('regions', 'gz'), 'gy'), parts along dimension 0, may hold values 0 or 1
Outputs:
- iterate_out: float32 [16, 32, 128, 256], P(None, ('regions', 'gz'), 'gy'), parts along dimension 1
- residual_out: float32 [16, 32, 128, 256], P(None, ('regions', 'gz'), 'gy'), parts along dimension 1
There are 2 independent parts, one for each index of `regions`. A program takes and returns all parts, laid end to end along the dimension named above; each array names one. Nothing has to cross between parts.
All inputs are finite; a program needn't handle non-finite values. No bound on the sum of `boundary` on one device may be relied on, other than what follows from the above.
Results may differ from a plain program's by a relative error of at most 0.0003.
Values sent between devices are 32-bit elements; how exact they have to be, the bound alone decides.
A program may use at most 128 MiB of HBM per device.

v0:
```python
import math
import jax
import jax.numpy as jnp
from jax import lax
from jax.sharding import PartitionSpec as P

NCLASS = 8
ITERS = 3
contrast_log = 4.0 * math.log(10.0)
highest = lax.Precision.HIGHEST


def extended_2(cells, sides, width):
    for axis, dim in sides:
        count = lax.axis_size(axis)
        ends = count - 1
        head = lax.slice_in_dim(cells, 0, width, axis=dim)
        tail = lax.slice_in_dim(cells, cells.shape[dim] - width, cells.shape[dim], axis=dim)
        cells = jnp.concatenate(
            [
                lax.ppermute(tail, axis, [(i, (i + 1) % count) for i in range(ends)]),
                cells,
                lax.ppermute(head, axis, [((i + 1) % count, i) for i in range(ends)]),
            ],
            axis=dim,
        )
    return cells


def shift_cells(block, forward):
    widths = [(0, 0)] * (block.ndim - 1)
    if forward:
        return jnp.pad(block[..., 1:], widths + [(0, 1)])
    return jnp.pad(block[..., :-1], widths + [(1, 0)])


def neighbors(extended):
    center = extended[..., 1:-1, 1:-1, :]
    beside = [
        extended[..., 2:, 1:-1, :],
        extended[..., :-2, 1:-1, :],
        extended[..., 1:-1, 2:, :],
        extended[..., 1:-1, :-2, :],
        shift_cells(center, True),
        shift_cells(center, False),
    ]
    return (center, beside)


def couplings_of(extended):
    coef_center, coef_beside = neighbors(extended[0])
    inner_center, inner_beside = neighbors(extended[1])
    diagonal = jnp.zeros_like(coef_center)
    offsets = []
    for neighbor_coef, neighbor_inner in zip(coef_beside, inner_beside):
        face_coef = jnp.where(
            neighbor_coef > 0.0,
            2.0 * coef_center * neighbor_coef / (coef_center + neighbor_coef),
            coef_center,
        )
        diagonal = diagonal + face_coef
        offsets.append(inner_center * face_coef * neighbor_inner)
    diagonal = inner_center * diagonal + (1.0 - inner_center)
    return (diagonal, offsets)


def apply_operator(diagonal, offsets, extended):
    center, beside = neighbors(extended)
    coupled = offsets[0] * beside[0]
    for weight, values in zip(offsets[1:], beside[1:]):
        coupled = coupled + weight * values
    return diagonal * center - coupled


def cell_fields(labels, boundary):
    coef = jnp.exp(labels.astype(jnp.float32) * (contrast_log / (NCLASS - 1)))
    interior = (1 - boundary).astype(jnp.float32)
    return jnp.stack([coef, interior])


def gram(left_block, right_block):
    left_flat = left_block.reshape(left_block.shape[0], -1)
    right_flat = right_block.reshape(right_block.shape[0], -1)
    return lax.dot_general(left_flat, right_flat, (((1,), (1,)), ((), ())), precision=highest)


def combine(block, weights):
    flat = block.reshape(block.shape[0], -1)
    mixed = lax.dot_general(weights, flat, (((0,), (0,)), ((), ())), precision=highest)
    return mixed.reshape(block.shape)


def spd_solve(matrix, right):
    factor = jnp.linalg.cholesky(matrix)
    return jax.scipy.linalg.cho_solve((factor, True), right)


def direction_cells(field):
    return extended_2(field, (("gz", 1), ("gy", 2)), 1)


def on_device(iterate, residual, labels, boundary):
    fields = cell_fields(labels, boundary)
    extended = extended_2(fields, (("gz", 1), ("gy", 2)), 1)
    diagonal, offsets = couplings_of(extended)
    inverse_diag = 1.0 / diagonal
    scaled = inverse_diag * residual
    direction = scaled
    for iteration in range(ITERS):
        direction_ext = direction_cells(direction)
        image = apply_operator(diagonal, offsets, direction_ext)
        weighted = inverse_diag * image
        summed_rho, curvature, cross_gram, image_gram = lax.psum(
            (
                gram(residual, scaled),
                gram(direction, image),
                gram(scaled, image),
                gram(image, weighted),
            ),
            ("gz", "gy"),
        )
        step_size = spd_solve(curvature, summed_rho)
        iterate = iterate + combine(direction, step_size)
        residual = residual - combine(image, step_size)
        if iteration + 1 < ITERS:
            scaled = inverse_diag * residual
            moved = jnp.dot(cross_gram, step_size, precision=highest)
            quadratic = jnp.dot(
                step_size.T, jnp.dot(image_gram, step_size, precision=highest), precision=highest
            )
            next_rho = summed_rho - moved - moved.T + quadratic
            momentum = spd_solve(summed_rho, next_rho)
            direction = scaled + combine(direction, momentum)
            summed_rho = next_rho
    return (iterate, residual)


def solution(mesh):
    placed = (
        P(None, ("regions", "gz"), "gy", None),
        P(None, ("regions", "gz"), "gy", None),
        P(("regions", "gz"), "gy", None),
        P(("regions", "gz"), "gy", None),
    )
    return jax.shard_map(
        on_device,
        mesh=mesh,
        in_specs=placed,
        out_specs=(P(None, ("regions", "gz"), "gy", None), P(None, ("regions", "gz"), "gy", None)),
        check_vma=False,
    )
```

profile of v0, /device:TPU:0, one launch (start us, length us, event | category | flops | bytes accessed | tf_op | source)
XLA Modules:
  0.0 462.8 jit_solution(4175048000201397154)
XLA Ops:
  2.5 1.3 collective-permute-start.1
  3.8 5.5 %collective-permute-start = (f32[2,1,64,256]{3,2,1,0:T(8,128)S(1)}, f32[2,1,64,256]{3,2,1,0:T(8,128)S(1)}, u32[]{:S(2)}, u32[]{:S(2)}) collective-permute-start(f32[2,1,64,256]{3,2,1,0:T(8,128)S(1)} %get-tuple-element.51), channel_id=1, source_target_pairs={{0,2},{2,4},{4,6},{6,8},{8,10},{10,12},{12,14},{1,3},{3,5},{5,7},{... | collective-permute-start | bytes 393224 | tf_op jit(solution)/shard_map/ppermute | solution.py:21
  9.3 1.5 collective-permute-done.1
  10.9 3.0 collective-permute-done
  13.9 1.3 collective-permute-start.3
  15.2 3.0 collective-permute-start.2
  22.1 1.3 collective-permute-start.4
  23.4 5.1 %collective-permute-start.5 = (f32[16,1,64,256]{3,0,2,1:T(8,128)S(1)}, f32[16,1,64,256]{3,0,2,1:T(8,128)S(1)}, u32[]{:S(2)}, u32[]{:S(2)}) collective-permute-start(f32[16,1,64,256]{3,0,2,1:T(8,128)S(1)} %get-tuple-element.35), channel_id=1, source_target_pairs={{0,2},{2,4},{4,6},{6,8},{8,10},{10,12},{12,14},{1,3},{3,5},{5,7},{... | collective-permute-start | bytes 3145736 | tf_op jit(solution)/shard_map/ppermute | solution.py:21
  28.5 3.5 fusion.74
  32.7 17.4 %collective-permute-done.4 = f32[16,1,64,256]{3,0,2,1:T(8,128)S(1)} collective-permute-done((f32[16,1,64,256]{3,0,2,1:T(8,128)S(1)}, f32[16,1,64,256]{3,0,2,1:T(8,128)S(1)}, u32[]{:S(2)}, u32[]{:S(2)}) %collective-permute-start.4) | collective-permute-done | bytes 1048608 | tf_op jit(solution)/shard_map/ppermute | solution.py:23
  50.1 22.6 %collective-permute-done.5 = f32[16,1,64,256]{3,0,2,1:T(8,128)S(1)} collective-permute-done((f32[16,1,64,256]{3,0,2,1:T(8,128)S(1)}, f32[16,1,64,256]{3,0,2,1:T(8,128)S(1)}, u32[]{:S(2)}, u32[]{:S(2)}) %collective-permute-start.5) | collective-permute-done | bytes 1048608 | tf_op jit(solution)/shard_map/ppermute | solution.py:21
  72.8 1.9 collective-permute-start.7
  74.7 1.5 collective-permute-start.6
  76.4 2.5 copy.93
  79.0 3.2 fusion.34
  82.2 3.8 convolution_bitcast_fusion.5
  86.0 2.7 fusion.86
  88.8 2.6 copy.95
  91.3 60.9 %all-reduce.12 = (f32[16,16]{0,1:T(8,128)S(1)}, f32[16,16]{0,1:T(8,128)S(1)}, f32[16,16]{1,0:T(8,128)S(1)}) all-reduce(f32[16,16]{0,1:T(8,128)S(1)} %fusion.74, f32[16,16]{0,1:T(8,128)S(1)} %convolution_bitcast_fusion.5, f32[16,16]{1,0:T(8,128)S(1)} %fusion.86), channel_id=1, replica_groups=mesh['regions'=2,'gz'=8,'gy'=2] {'gz','gy'}, use_global_device_ids=true, to_apply=%region_3.5 | all-reduce | flops 768 | bytes 6144 | tf_op jit(solution)/shard_map/psum | solution.py:113
  152.3 1.5 cholesky.89
  155.2 1.2 custom-call.11
  157.0 6.3 %copy_subtract_fusion = f32[16,2,64,256]{3,0,2,1:T(8,128)S(1)} fusion(f32[16,2,64,256]{3,2,1,0:T(8,128)} %param.8, f32[2,64,256,16]{2,1,0,3:T(8,128)} %bitcast.241, f32[16,16]{1,0:T(8,128)S(1)} %fusion.124), kind=kOutput, calls=%fused_computation.85 | convolution fusion | flops 101187584 | bytes 6292480 | tf_op jit(solution)/shard_map/dot_general | solution.py:89
  163.5 1.5 cholesky.100
  166.3 1.2 custom-call.12
  168.1 4.5 multiply_add_fusion.1
  172.8 1.3 collective-permute-start.8
  174.1 4.6 collective-permute-start.9
  179.5 15.8 %collective-permute-done.8 = f32[16,1,64,256]{3,0,2,1:T(8,128)S(1)} collective-permute-done((f32[16,1,64,256]{3,0,2,1:T(8,128)S(1)}, f32[16,1,64,256]{3,0,2,1:T(8,128)S(1)}, u32[]{:S(2)}, u32[]{:S(2)}) %collective-permute-start.8) | collective-permute-done | bytes 1048608 | tf_op jit(solution)/shard_map/ppermute | solution.py:23
  195.3 18.0 %collective-permute-done.9 = f32[16,1,64,256]{3,0,2,1:T(8,128)S(1)} collective-permute-done((f32[16,1,64,256]{3,0,2,1:T(8,128)S(1)}, f32[16,1,64,256]{3,0,2,1:T(8,128)S(1)}, u32[]{:S(2)}, u32[]{:S(2)}) %collective-permute-start.9) | collective-permute-done | bytes 1048608 | tf_op jit(solution)/shard_map/ppermute | solution.py:21
  213.2 1.9 collective-permute-start.11
  215.2 1.8 collective-permute-start.10
  216.9 2.8 fusion.77
  219.7 2.6 copy.97
  222.3 3.2 fusion.24
  225.5 2.9 convolution_bitcast_fusion.3
  228.4 2.8 fusion.89
  231.2 2.8 fusion.80
  234.0 2.6 copy.99
  236.6 62.6 %all-reduce.11 = (f32[16,16]{0,1:T(8,128)S(1)}, f32[16,16]{0,1:T(8,128)S(1)}, f32[16,16]{1,0:T(8,128)S(1)}, f32[16,16]{1,0:T(8,128)S(1)}) all-reduce(f32[16,16]{0,1:T(8,128)S(1)} %fusion.77, f32[16,16]{0,1:T(8,128)S(1)} %convolution_bitcast_fusion.3, f32[16,16]{1,0:T(8,128)S(1)} %fusion.89, ...), channel_id=1, replica_groups=mesh['regions'=2,'gz'=8,'gy'=2] {'gz','gy'}, use_global_device_ids=true, to_apply=%region_6.9 | all-reduce | flops 1024 | bytes 8192 | tf_op jit(solution)/shard_map/psum | solution.py:113
  299.2 1.5 cholesky.111
  301.9 1.2 custom-call.13
  303.5 5.7 %fusion.68 = f32[16,2,64,256]{3,0,2,1:T(8,128)} fusion(f32[16,2,64,256]{3,0,2,1:T(8,128)S(1)} %copy_subtract_fusion, f32[2,64,256,16]{2,1,0,3:T(8,128)} %bitcast.240, f32[16,16]{1,0:T(8,128)S(1)} %fusion.113), kind=kOutput, calls=%fused_computation.89 | convolution fusion | flops 101187584 | bytes 6292480 | tf_op jit(solution)/shard_map/dot_general | solution.py:89
  309.5 1.5 cholesky.122
  312.3 1.2 custom-call.14
  314.1 5.2 %multiply_add_fusion = f32[16,2,64,256]{3,0,2,1:T(8,128)S(1)} fusion(f32[16,2,64,256]{3,0,2,1:T(8,128)} %fusion.68, f32[16,16,1,1]{0,1,3,2:T(8,128)S(1)} %convolution_bitcast_fusion.2, f32[2,64,256,16]{2,1,0,3:T(8,128)} %bitcast.234, f32[2,64,256]{2,1,0:T(8,128)S(1)} %get-tuple-element.17), kind=kOutput, calls=%fused_computation.6 | convolution fusion | flops 101711872 | bytes 6423552 | tf_op jit(solution)/shard_map/dot_general | solution.py:89
  319.5 1.4 collective-permute-start.12
  320.9 4.6 collective-permute-start.13
  325.6 4.2 fusion.52
  330.5 11.6 %collective-permute-done.12 = f32[16,1,64,256]{3,0,2,1:T(8,128)S(1)} collective-permute-done((f32[16,1,64,256]{3,0,2,1:T(8,128)S(1)}, f32[16,1,64,256]{3,0,2,1:T(8,128)S(1)}, u32[]{:S(2)}, u32[]{:S(2)}) %collective-permute-start.12) | collective-permute-done | bytes 1048608 | tf_op jit(solution)/shard_map/ppermute | solution.py:23
  342.1 18.0 %collective-permute-done.13 = f32[16,1,64,256]{3,0,2,1:T(8,128)S(1)} collective-permute-done((f32[16,1,64,256]{3,0,2,1:T(8,128)S(1)}, f32[16,1,64,256]{3,0,2,1:T(8,128)S(1)}, u32[]{:S(2)}, u32[]{:S(2)}) %collective-permute-start.13) | collective-permute-done | bytes 1048608 | tf_op jit(solution)/shard_map/ppermute | solution.py:21
  360.0 1.9 collective-permute-start.15
  362.0 1.3 collective-permute-start.14
  363.3 2.7 fusion.83
  366.0 2.6 copy.101
  368.6 3.2 fusion.14
  371.8 1.3 copy-done.4
  373.1 2.9 convolution_bitcast_fusion.1
  376.0 62.5 %all-reduce.10 = (f32[16,16]{1,0:T(8,128)S(1)}, f32[16,16]{0,1:T(8,128)S(1)}) all-reduce(f32[16,16]{1,0:T(8,128)S(1)} %fusion.83, f32[16,16]{0,1:T(8,128)S(1)} %convolution_bitcast_fusion.1), channel_id=1, replica_groups=mesh['regions'=2,'gz'=8,'gy'=2] {'gz','gy'}, use_global_device_ids=true, to_apply=%region_10.13 | all-reduce | flops 512 | bytes 4096 | tf_op jit(solution)/shard_map/psum | solution.py:113
  438.6 1.5 cholesky.133
  442.9 4.5 fusion.42
  447.5 5.7 %fusion.49 = f32[16,2,64,256]{3,0,2,1:T(8,128)S(1)} fusion(f32[16,2,64,256]{3,0,2,1:T(8,128)S(1)} %fusion.42, f32[16,2,64,256]{3,0,2,1:T(8,128)S(1)} %copy-done.6, f32[16,2,64,256]{3,2,1,0:T(8,128)} %param.7, f32[2,64,256,16]{2,1,0,3:T(8,128)S(1)} %bitcast.237, f32[16,16]{1,0:T(8,128)S(1)} %fusion.124), kind=kOutput, calls=%fused_computation.76 | convolution fusion | flops 102236160 | bytes 10486784 | tf_op jit(solution)/shard_map/dot_general | solution.py:89
  453.2 2.5 copy.64
  457.0 2.9 fusion.71
  459.8 2.5 copy.65
  (85 shorter events, 20.9 us)
Async XLA Ops:
  2.5 8.4 %collective-permute-start.1 = (f32[2,1,64,256]{3,2,1,0:T(8,128)S(1)}, f32[2,1,64,256]{3,2,1,0:T(8,128)S(1)}, u32[]{:S(2)}, u32[]{:S(2)}) collective-permute-start(f32[2,1,64,256]{3,2,1,0:T(8,128)S(1)} %get-tuple-element.52), channel_id=1, source_target_pairs={{2,0},{4,2},{6,4},{8,6},{10,8},{12,10},{14,12},{3,1},{5,3},{7,5},{... | collective-permute-start | bytes 393224 | tf_op jit(solution)/shard_map/ppermute | solution.py:23
  3.8 10.0 %collective-permute-start = (f32[2,1,64,256]{3,2,1,0:T(8,128)S(1)}, f32[2,1,64,256]{3,2,1,0:T(8,128)S(1)}, u32[]{:S(2)}, u32[]{:S(2)}) collective-permute-start(f32[2,1,64,256]{3,2,1,0:T(8,128)S(1)} %get-tuple-element.51), channel_id=1, source_target_pairs={{0,2},{2,4},{4,6},{6,8},{8,10},{10,12},{12,14},{1,3},{3,5},{5,7},{... | collective-permute-start | bytes 393224 | tf_op jit(solution)/shard_map/ppermute | solution.py:21
  13.9 4.3 collective-permute-start.3
  15.2 3.8 collective-permute-start.2
  19.1 1.6 copy-start
  22.1 28.1 %collective-permute-start.4 = (f32[16,1,64,256]{3,0,2,1:T(8,128)S(1)}, f32[16,1,64,256]{3,0,2,1:T(8,128)S(1)}, u32[]{:S(2)}, u32[]{:S(2)}) collective-permute-start(f32[16,1,64,256]{3,0,2,1:T(8,128)S(1)} %get-tuple-element.36), channel_id=1, source_target_pairs={{2,0},{4,2},{6,4},{8,6},{10,8},{12,10},{14,12},{3,1},{5,3},{7,5},{... | collective-permute-start | bytes 3145736 | tf_op jit(solution)/shard_map/ppermute | solution.py:23
  23.4 49.4 %collective-permute-start.5 = (f32[16,1,64,256]{3,0,2,1:T(8,128)S(1)}, f32[16,1,64,256]{3,0,2,1:T(8,128)S(1)}, u32[]{:S(2)}, u32[]{:S(2)}) collective-permute-start(f32[16,1,64,256]{3,0,2,1:T(8,128)S(1)} %get-tuple-element.35), channel_id=1, source_target_pairs={{0,2},{2,4},{4,6},{6,8},{8,10},{10,12},{12,14},{1,3},{3,5},{5,7},{... | collective-permute-start | bytes 3145736 | tf_op jit(solution)/shard_map/ppermute | solution.py:21
  72.8 6.2 %collective-permute-start.7 = (f32[16,4,1,256]{3,0,2,1:T(8,128)S(1)}, f32[16,4,1,256]{3,0,2,1:T(8,128)S(1)}, u32[]{:S(2)}, u32[]{:S(2)}) collective-permute-start(f32[16,4,1,256]{3,0,2,1:T(8,128)S(1)} %get-tuple-element.24), channel_id=1, source_target_pairs={{0,1},{2,3},{4,5},{6,7},{8,9},{10,11},{12,13},{14,15},{16,17},{18,... | collective-permute-start | bytes 196616 | tf_op jit(solution)/shard_map/ppermute | solution.py:21
  74.7 4.3 collective-permute-start.6
  172.8 22.4 %collective-permute-start.8 = (f32[16,1,64,256]{3,0,2,1:T(8,128)S(1)}, f32[16,1,64,256]{3,0,2,1:T(8,128)S(1)}, u32[]{:S(2)}, u32[]{:S(2)}) collective-permute-start(f32[16,1,64,256]{3,0,2,1:T(8,128)S(1)} %get-tuple-element.32), channel_id=1, source_target_pairs={{2,0},{4,2},{6,4},{8,6},{10,8},{12,10},{14,12},{3,1},{5,3},{7,5},{... | collective-permute-start | bytes 3145736 | tf_op jit(solution)/shard_map/ppermute | solution.py:23
  174.1 39.1 %collective-permute-start.9 = (f32[16,1,64,256]{3,0,2,1:T(8,128)S(1)}, f32[16,1,64,256]{3,0,2,1:T(8,128)S(1)}, u32[]{:S(2)}, u32[]{:S(2)}) collective-permute-start(f32[16,1,64,256]{3,0,2,1:T(8,128)S(1)} %get-tuple-element.31), channel_id=1, source_target_pairs={{0,2},{2,4},{4,6},{6,8},{8,10},{10,12},{12,14},{1,3},{3,5},{5,7},{... | collective-permute-start | bytes 3145736 | tf_op jit(solution)/shard_map/ppermute | solution.py:21
  213.2 9.0 %collective-permute-start.11 = (f32[16,4,1,256]{3,0,2,1:T(8,128)S(1)}, f32[16,4,1,256]{3,0,2,1:T(8,128)S(1)}, u32[]{:S(2)}, u32[]{:S(2)}) collective-permute-start(f32[16,4,1,256]{3,0,2,1:T(8,128)S(1)} %get-tuple-element.22), channel_id=1, source_target_pairs={{0,1},{2,3},{4,5},{6,7},{8,9},{10,11},{12,13},{14,15},{16,17},{18,... | collective-permute-start | bytes 196616 | tf_op jit(solution)/shard_map/ppermute | solution.py:21
  215.2 7.1 %collective-permute-start.10 = (f32[16,4,1,256]{3,0,2,1:T(8,128)S(1)}, f32[16,4,1,256]{3,0,2,1:T(8,128)S(1)}, u32[]{:S(2)}, u32[]{:S(2)}) collective-permute-start(f32[16,4,1,256]{3,0,2,1:T(8,128)S(1)} %get-tuple-element.21), channel_id=1, source_target_pairs={{1,0},{3,2},{5,4},{7,6},{9,8},{11,10},{13,12},{15,14},{17,16},{19,... | collective-permute-start | bytes 196616 | tf_op jit(solution)/shard_map/ppermute | solution.py:23
  319.3 6.2 %copy-start.2 = (f32[2,8,128,256]{3,2,1,0:T(8,128)S(1)}, f32[2,8,128,256]{3,2,1,0:T(8,128)}, u32[]{:S(2)}) copy-start(f32[2,8,128,256]{3,2,1,0:T(8,128)} %copy.97) | copy-start | bytes 6291460
  319.5 22.6 %collective-permute-start.12 = (f32[16,1,64,256]{3,0,2,1:T(8,128)S(1)}, f32[16,1,64,256]{3,0,2,1:T(8,128)S(1)}, u32[]{:S(2)}, u32[]{:S(2)}) collective-permute-start(f32[16,1,64,256]{3,0,2,1:T(8,128)S(1)} %get-tuple-element.28), channel_id=1, source_target_pairs={{2,0},{4,2},{6,4},{8,6},{10,8},{12,10},{14,12},{3,1},{5,3},{7,5},{... | collective-permute-start | bytes 3145736 | tf_op jit(solution)/shard_map/ppermute | solution.py:23
  320.9 39.1 %collective-permute-start.13 = (f32[16,1,64,256]{3,0,2,1:T(8,128)S(1)}, f32[16,1,64,256]{3,0,2,1:T(8,128)S(1)}, u32[]{:S(2)}, u32[]{:S(2)}) collective-permute-start(f32[16,1,64,256]{3,0,2,1:T(8,128)S(1)} %get-tuple-element.27), channel_id=1, source_target_pairs={{0,2},{2,4},{4,6},{6,8},{8,10},{10,12},{12,14},{1,3},{3,5},{5,7},{... | collective-permute-start | bytes 3145736 | tf_op jit(solution)/shard_map/ppermute | solution.py:21
  330.5 32.8 %copy-start.1 = (f32[16,2,64,256]{3,0,2,1:T(8,128)S(1)}, f32[16,2,64,256]{3,0,2,1:T(8,128)}, u32[]{:S(2)}) copy-start(f32[16,2,64,256]{3,0,2,1:T(8,128)} %fusion.68) | copy-start | bytes 6291460
  360.0 8.5 %collective-permute-start.15 = (f32[16,4,1,256]{3,0,2,1:T(8,128)S(1)}, f32[16,4,1,256]{3,0,2,1:T(8,128)S(1)}, u32[]{:S(2)}, u32[]{:S(2)}) collective-permute-start(f32[16,4,1,256]{3,0,2,1:T(8,128)S(1)} %get-tuple-element.20), channel_id=1, source_target_pairs={{0,1},{2,3},{4,5},{6,7},{8,9},{10,11},{12,13},{14,15},{16,17},{18,... | collective-permute-start | bytes 196616 | tf_op jit(solution)/shard_map/ppermute | solution.py:21
  362.0 6.6 %collective-permute-start.14 = (f32[16,4,1,256]{3,0,2,1:T(8,128)S(1)}, f32[16,4,1,256]{3,0,2,1:T(8,128)S(1)}, u32[]{:S(2)}, u32[]{:S(2)}) collective-permute-start(f32[16,4,1,256]{3,0,2,1:T(8,128)S(1)} %get-tuple-element.19), channel_id=1, source_target_pairs={{1,0},{3,2},{5,4},{7,6},{9,8},{11,10},{13,12},{15,14},{17,16},{19,... | collective-permute-start | bytes 196616 | tf_op jit(solution)/shard_map/ppermute | solution.py:23
  371.8 1.3 copy-start.4
  442.9 4.6 copy-start.3
  442.9 4.6 copy-start.6
  453.2 2.5 copy-start.5
where the time goes:
time: 469 us; the launch traced here: 463 us
  blocking collectives  186 us (40%)
  waiting for transfers between devices  109 us (23%)
  matrix products  68.6 us (15%)
  starting transfers between devices  39.8 us (8%)
  other arithmetic  33.3 us (7%)
  local copies, waits for them, and re-layouts  24.9 us (5%)
    psum x3, blocking collectives, on_device(): lax.psum((gram(residual, scaled), gram(direction, image), gram(scaled, im...  186 us
    ppermute x8, waiting for transfers between devices, extended_2(): lax.ppermute(tail, axis, [(i, (i + 1) % count) for i in range(ends)])  62.3 us
    ppermute x8, waiting for transfers between devices, extended_2(): lax.ppermute(head, axis, [((i + 1) % count, i) for i in range(ends)])  46.3 us
    dot_general x8, matrix products, combine(): lax.dot_general(weights, flat, (((0,), (0,)), ((), ())), precision=highest)  38.9 us
    ppermute x8, starting transfers between devices, extended_2(): lax.ppermute(tail, axis, [(i, (i + 1) % count) for i in range(ends)])  28.6 us
    dot_general x9, matrix products, gram(): lax.dot_general(left_flat, right_flat, (((1,), (1,)), ((), ())), precisio...  26.8 us
    unnamed x22, local copies, waits for them, and re-layouts  21.5 us
    ppermute x8, starting transfers between devices, extended_2(): lax.ppermute(head, axis, [((i + 1) % count, i) for i in range(ends)])  11.1 us
  transfers between devices with their start and end apart: 16, of which 9 were waited for; matrix products, arithmetic and copies ran while one was open for 5% of the time, Pallas kernels for 0%

commit v1 on v0

--- a/solution.py
+++ b/solution.py
@@ -111,13 +111,16 @@
         image = apply_operator(diagonal, offsets, direction_ext)
         weighted = inverse_diag * image
         summed_rho, curvature, cross_gram, image_gram = lax.psum(
-            (
-                gram(residual, scaled),
-                gram(direction, image),
-                gram(scaled, image),
-                gram(image, weighted),
+            lax.psum(
+                (
+                    gram(residual, scaled),
+                    gram(direction, image),
+                    gram(scaled, image),
+                    gram(image, weighted),
+                ),
+                "gz",
             ),
-            ("gz", "gy"),
+            "gy",
         )
         step_size = spd_solve(curvature, summed_rho)
         iterate = iterate + combine(direction, step_size)

time: 469 us -> 411 us (0.88)
  blocking collectives: 186 us -> 117 us
  waiting for transfers between devices: 109 us -> 119 us
    psum x3, blocking collectives: 186 us -> 106 us  [on_device(): lax.psum((gram(residual, scaled), gram(direction, image), gram(scaled, im...]
    psum x0 -> x3, blocking collectives: none -> 10.8 us  [on_device(): lax.psum(lax.psum((gram(residual, scaled), gram(direction, image), gram(s...]
    ppermute x8, waiting for transfers between devices: 46.3 us -> 56 us  [extended_2(): lax.ppermute(head, axis, [((i + 1) % count, i) for i in range(ends)])]
  transfers between devices with their start and end apart: 16 -> 16, of which waited for: 9 -> 9; matrix products, arithmetic and copies ran while one was open for 5% -> 6% of each run, Pallas kernels for 0% -> 0%
where the time goes in v1:
time: 411 us; the launch traced here: 405 us
  waiting for transfers between devices  119 us (29%)
  blocking collectives  117 us (28%)
  matrix products  68.6 us (17%)
  starting transfers between devices  39.9 us (10%)
  other arithmetic  33.6 us (8%)
  local copies, waits for them, and re-layouts  24.9 us (6%)
    psum x3, blocking collectives, on_device(): lax.psum((gram(residual, scaled), gram(direction, image), gram(scaled, im...  106 us
    ppermute x8, waiting for transfers between devices, extended_2(): lax.ppermute(tail, axis, [(i, (i + 1) % count) for i in range(ends)])  63.4 us
    ppermute x8, waiting for transfers between devices, extended_2(): lax.ppermute(head, axis, [((i + 1) % count, i) for i in range(ends)])  56 us
    dot_general x8, matrix products, combine(): lax.dot_general(weights, flat, (((0,), (0,)), ((), ())), precision=highest)  38.8 us
    ppermute x8, starting transfers between devices, extended_2(): lax.ppermute(tail, axis, [(i, (i + 1) % count) for i in range(ends)])  28.7 us
    dot_general x9, matrix products, gram(): lax.dot_general(left_flat, right_flat, (((1,), (1,)), ((), ())), precisio...  26.9 us
    unnamed x22, local copies, waits for them, and re-layouts  21.5 us
    ppermute x8, starting transfers between devices, extended_2(): lax.ppermute(head, axis, [((i + 1) % count, i) for i in range(ends)])  11.2 us
  transfers between devices with their start and end apart: 16, of which 9 were waited for; matrix products, arithmetic and copies ran while one was open for 6% of the time, Pallas kernels for 0%

profile of v1, /device:TPU:0, one launch (start us, length us, event | category | flops | bytes accessed | tf_op | source)
XLA Modules:
  0.0 404.9 jit_solution(16656962548604108977)
XLA Ops:
  2.5 1.3 collective-permute-start.1
  3.8 5.5 %collective-permute-start = (f32[2,1,64,256]{3,2,1,0:T(8,128)S(1)}, f32[2,1,64,256]{3,2,1,0:T(8,128)S(1)}, u32[]{:S(2)}, u32[]{:S(2)}) collective-permute-start(f32[2,1,64,256]{3,2,1,0:T(8,128)S(1)} %get-tuple-element.60), channel_id=1, source_target_pairs={{0,2},{2,4},{4,6},{6,8},{8,10},{10,12},{12,14},{1,3},{3,5},{5,7},{... | collective-permute-start | bytes 393224 | tf_op jit(solution)/shard_map/ppermute | solution.py:21
  9.3 1.5 collective-permute-done.1
  10.9 3.0 collective-permute-done
  13.9 1.3 collective-permute-start.3
  15.2 3.0 collective-permute-start.2
  22.1 1.3 collective-permute-start.4
  23.4 5.1 %collective-permute-start.5 = (f32[16,1,64,256]{3,0,2,1:T(8,128)S(1)}, f32[16,1,64,256]{3,0,2,1:T(8,128)S(1)}, u32[]{:S(2)}, u32[]{:S(2)}) collective-permute-start(f32[16,1,64,256]{3,0,2,1:T(8,128)S(1)} %get-tuple-element.44), channel_id=1, source_target_pairs={{0,2},{2,4},{4,6},{6,8},{8,10},{10,12},{12,14},{1,3},{3,5},{5,7},{... | collective-permute-start | bytes 3145736 | tf_op jit(solution)/shard_map/ppermute | solution.py:21
  28.5 3.5 fusion.74
  32.7 17.4 %collective-permute-done.4 = f32[16,1,64,256]{3,0,2,1:T(8,128)S(1)} collective-permute-done((f32[16,1,64,256]{3,0,2,1:T(8,128)S(1)}, f32[16,1,64,256]{3,0,2,1:T(8,128)S(1)}, u32[]{:S(2)}, u32[]{:S(2)}) %collective-permute-start.4) | collective-permute-done | bytes 1048608 | tf_op jit(solution)/shard_map/ppermute | solution.py:23
  50.1 22.6 %collective-permute-done.5 = f32[16,1,64,256]{3,0,2,1:T(8,128)S(1)} collective-permute-done((f32[16,1,64,256]{3,0,2,1:T(8,128)S(1)}, f32[16,1,64,256]{3,0,2,1:T(8,128)S(1)}, u32[]{:S(2)}, u32[]{:S(2)}) %collective-permute-start.5) | collective-permute-done | bytes 1048608 | tf_op jit(solution)/shard_map/ppermute | solution.py:21
  72.8 1.9 collective-permute-start.7
  74.7 1.5 collective-permute-start.6
  76.4 2.5 copy.93
  79.0 3.2 fusion.34
  82.2 3.8 convolution_bitcast_fusion.5
  86.0 2.7 fusion.86
  88.8 2.6 copy.95
  91.3 35.6 %all-reduce.12 = (f32[16,16]{0,1:T(8,128)S(1)}, f32[16,16]{0,1:T(8,128)S(1)}, f32[16,16]{1,0:T(8,128)S(1)}) all-reduce(f32[16,16]{0,1:T(8,128)S(1)} %fusion.74, f32[16,16]{0,1:T(8,128)S(1)} %convolution_bitcast_fusion.5, f32[16,16]{1,0:T(8,128)S(1)} %fusion.86), channel_id=1, replica_groups=mesh['regions'=2,'gz'=8,'gy'=2] {'gz'}, use_global_device_ids=true, to_apply=%region_4.6 | all-reduce | flops 768 | bytes 6144 | tf_op jit(solution)/shard_map/psum | solution.py:114
  126.9 3.7 all-reduce.15
  130.7 1.5 cholesky.89
  133.6 1.2 custom-call.11
  135.4 6.3 %copy_subtract_fusion = f32[16,2,64,256]{3,0,2,1:T(8,128)S(1)} fusion(f32[16,2,64,256]{3,2,1,0:T(8,128)} %param.8, f32[2,64,256,16]{2,1,0,3:T(8,128)} %bitcast.241, f32[16,16]{1,0:T(8,128)S(1)} %fusion.124), kind=kOutput, calls=%fused_computation.85 | convolution fusion | flops 101187584 | bytes 6292480 | tf_op jit(solution)/shard_map/dot_general | solution.py:89
  141.9 1.5 cholesky.100
  146.5 4.5 %multiply_add_fusion.1 = f32[16,2,64,256]{3,0,2,1:T(8,128)S(1)} fusion(f32[16,2,64,256]{3,0,2,1:T(8,128)S(1)} %copy_subtract_fusion, f32[16,16,1,1]{0,1,3,2:T(8,128)S(1)} %convolution_bitcast_fusion.4, f32[2,64,256,16]{2,1,0,3:T(8,128)} %bitcast.236, f32[2,64,256]{2,1,0:T(8,128)S(1)} %get-tuple-element.26), kind=kOutput, calls=%fused_computation.11 | convolution fusion | flops 101711872 | bytes 6423552 | tf_op jit(solution)/shard_map/dot_general | solution.py:89
  151.2 1.3 collective-permute-start.8
  152.5 4.6 %collective-permute-start.9 = (f32[16,1,64,256]{3,0,2,1:T(8,128)S(1)}, f32[16,1,64,256]{3,0,2,1:T(8,128)S(1)}, u32[]{:S(2)}, u32[]{:S(2)}) collective-permute-start(f32[16,1,64,256]{3,0,2,1:T(8,128)S(1)} %get-tuple-element.40), channel_id=1, source_target_pairs={{0,2},{2,4},{4,6},{6,8},{8,10},{10,12},{12,14},{1,3},{3,5},{5,7},{... | collective-permute-start | bytes 3145736 | tf_op jit(solution)/shard_map/ppermute | solution.py:21
  157.9 20.6 %collective-permute-done.8 = f32[16,1,64,256]{3,0,2,1:T(8,128)S(1)} collective-permute-done((f32[16,1,64,256]{3,0,2,1:T(8,128)S(1)}, f32[16,1,64,256]{3,0,2,1:T(8,128)S(1)}, u32[]{:S(2)}, u32[]{:S(2)}) %collective-permute-start.8) | collective-permute-done | bytes 1048608 | tf_op jit(solution)/shard_map/ppermute | solution.py:23
  178.5 18.5 %collective-permute-done.9 = f32[16,1,64,256]{3,0,2,1:T(8,128)S(1)} collective-permute-done((f32[16,1,64,256]{3,0,2,1:T(8,128)S(1)}, f32[16,1,64,256]{3,0,2,1:T(8,128)S(1)}, u32[]{:S(2)}, u32[]{:S(2)}) %collective-permute-start.9) | collective-permute-done | bytes 1048608 | tf_op jit(solution)/shard_map/ppermute | solution.py:21
  197.0 1.9 collective-permute-start.11
  199.0 1.8 collective-permute-start.10
  200.8 2.8 fusion.77
  203.6 2.6 copy.97
  206.2 3.2 fusion.24
  209.4 2.9 convolution_bitcast_fusion.3
  212.3 2.8 fusion.89
  215.1 2.8 fusion.80
  217.9 2.6 copy.99
  220.4 35.3 %all-reduce.11 = (f32[16,16]{0,1:T(8,128)S(1)}, f32[16,16]{0,1:T(8,128)S(1)}, f32[16,16]{1,0:T(8,128)S(1)}, f32[16,16]{1,0:T(8,128)S(1)}) all-reduce(f32[16,16]{0,1:T(8,128)S(1)} %fusion.77, f32[16,16]{0,1:T(8,128)S(1)} %convolution_bitcast_fusion.3, f32[16,16]{1,0:T(8,128)S(1)} %fusion.89, ...), channel_id=1, replica_groups=mesh['regions'=2,'gz'=8,'gy'=2] {'gz'}, use_global_device_ids=true, to_apply=%region_10.13 | all-reduce | flops 1024 | bytes 8192 | tf_op jit(solution)/shard_map/psum | solution.py:114
  255.8 3.6 all-reduce.14
  259.5 1.5 cholesky.111
  263.9 5.6 %fusion.68 = f32[16,2,64,256]{3,0,2,1:T(8,128)} fusion(f32[16,2,64,256]{3,0,2,1:T(8,128)S(1)} %copy_subtract_fusion, f32[2,64,256,16]{2,1,0,3:T(8,128)} %bitcast.240, f32[16,16]{1,0:T(8,128)S(1)} %fusion.113), kind=kOutput, calls=%fused_computation.89 | convolution fusion | flops 101187584 | bytes 6292480 | tf_op jit(solution)/shard_map/dot_general | solution.py:89
  269.9 1.5 cholesky.122
  274.5 5.2 %multiply_add_fusion = f32[16,2,64,256]{3,0,2,1:T(8,128)S(1)} fusion(f32[16,2,64,256]{3,0,2,1:T(8,128)} %fusion.68, f32[16,16,1,1]{0,1,3,2:T(8,128)S(1)} %convolution_bitcast_fusion.2, f32[2,64,256,16]{2,1,0,3:T(8,128)} %bitcast.234, f32[2,64,256]{2,1,0:T(8,128)S(1)} %get-tuple-element.26), kind=kOutput, calls=%fused_computation.6 | convolution fusion | flops 101711872 | bytes 6423552 | tf_op jit(solution)/shard_map/dot_general | solution.py:89
  279.9 1.4 collective-permute-start.12
  281.3 4.6 %collective-permute-start.13 = (f32[16,1,64,256]{3,0,2,1:T(8,128)S(1)}, f32[16,1,64,256]{3,0,2,1:T(8,128)S(1)}, u32[]{:S(2)}, u32[]{:S(2)}) collective-permute-start(f32[16,1,64,256]{3,0,2,1:T(8,128)S(1)} %get-tuple-element.36), channel_id=1, source_target_pairs={{0,2},{2,4},{4,6},{6,8},{8,10},{10,12},{12,14},{1,3},{3,5},{5,7},{... | collective-permute-start | bytes 3145736 | tf_op jit(solution)/shard_map/ppermute | solution.py:21
  285.9 4.2 %fusion.52 = f32[16,2,64,256]{3,0,2,1:T(8,128)} fusion(f32[2,64,256,16]{2,1,0,3:T(8,128)S(1)} %bitcast.235, f32[16,16]{1,0:T(8,128)S(1)} %fusion.113), kind=kOutput, calls=%fused_computation.79 | convolution fusion | flops 100663296 | bytes 4195328 | tf_op jit(solution)/shard_map/dot_general | solution.py:89
  290.9 16.4 %collective-permute-done.12 = f32[16,1,64,256]{3,0,2,1:T(8,128)S(1)} collective-permute-done((f32[16,1,64,256]{3,0,2,1:T(8,128)S(1)}, f32[16,1,64,256]{3,0,2,1:T(8,128)S(1)}, u32[]{:S(2)}, u32[]{:S(2)}) %collective-permute-start.12) | collective-permute-done | bytes 1048608 | tf_op jit(solution)/shard_map/ppermute | solution.py:23
  307.3 18.5 %collective-permute-done.13 = f32[16,1,64,256]{3,0,2,1:T(8,128)S(1)} collective-permute-done((f32[16,1,64,256]{3,0,2,1:T(8,128)S(1)}, f32[16,1,64,256]{3,0,2,1:T(8,128)S(1)}, u32[]{:S(2)}, u32[]{:S(2)}) %collective-permute-start.13) | collective-permute-done | bytes 1048608 | tf_op jit(solution)/shard_map/ppermute | solution.py:21
  325.8 1.9 collective-permute-start.15
  327.8 1.3 collective-permute-start.14
  329.1 2.7 fusion.83
  331.8 2.6 copy.101
  334.3 3.2 fusion.14
  337.6 1.3 copy-done.4
  338.9 2.9 convolution_bitcast_fusion.1
  341.8 35.4 %all-reduce.10 = (f32[16,16]{1,0:T(8,128)S(1)}, f32[16,16]{0,1:T(8,128)S(1)}) all-reduce(f32[16,16]{1,0:T(8,128)S(1)} %fusion.83, f32[16,16]{0,1:T(8,128)S(1)} %convolution_bitcast_fusion.1), channel_id=1, replica_groups=mesh['regions'=2,'gz'=8,'gy'=2] {'gz'}, use_global_device_ids=true, to_apply=%region_18.21 | all-reduce | flops 512 | bytes 4096 | tf_op jit(solution)/shard_map/psum | solution.py:114
  377.2 3.5 all-reduce.13
  380.7 1.5 cholesky.133
  385.1 4.5 %fusion.42 = f32[16,2,64,256]{3,0,2,1:T(8,128)S(1)} fusion(f32[16,16,1,1]{0,1,3,2:T(8,128)S(1)} %convolution_bitcast_fusion, f32[2,64,256,16]{2,1,0,3:T(8,128)} %bitcast.239), kind=kOutput, calls=%fused_computation.68 | convolution fusion | flops 100663296 | bytes 4195328 | tf_op jit(solution)/shard_map/dot_general | solution.py:89
  389.7 5.7 %fusion.49 = f32[16,2,64,256]{3,0,2,1:T(8,128)S(1)} fusion(f32[16,2,64,256]{3,0,2,1:T(8,128)S(1)} %fusion.42, f32[16,2,64,256]{3,0,2,1:T(8,128)S(1)} %copy-done.6, f32[16,2,64,256]{3,2,1,0:T(8,128)} %param.7, f32[2,64,256,16]{2,1,0,3:T(8,128)S(1)} %bitcast.237, f32[16,16]{1,0:T(8,128)S(1)} %fusion.124), kind=kOutput, calls=%fused_computation.76 | convolution fusion | flops 102236160 | bytes 10486784 | tf_op jit(solution)/shard_map/dot_general | solution.py:89
  395.4 2.5 copy.64
  399.1 2.9 fusion.71
  402.0 2.5 copy.65
  (88 shorter events, 24.8 us)
Async XLA Ops:
  2.5 8.4 %collective-permute-start.1 = (f32[2,1,64,256]{3,2,1,0:T(8,128)S(1)}, f32[2,1,64,256]{3,2,1,0:T(8,128)S(1)}, u32[]{:S(2)}, u32[]{:S(2)}) collective-permute-start(f32[2,1,64,256]{3,2,1,0:T(8,128)S(1)} %get-tuple-element.61), channel_id=1, source_target_pairs={{2,0},{4,2},{6,4},{8,6},{10,8},{12,10},{14,12},{3,1},{5,3},{7,5},{... | collective-permute-start | bytes 393224 | tf_op jit(solution)/shard_map/ppermute | solution.py:23
  3.8 10.0 %collective-permute-start = (f32[2,1,64,256]{3,2,1,0:T(8,128)S(1)}, f32[2,1,64,256]{3,2,1,0:T(8,128)S(1)}, u32[]{:S(2)}, u32[]{:S(2)}) collective-permute-start(f32[2,1,64,256]{3,2,1,0:T(8,128)S(1)} %get-tuple-element.60), channel_id=1, source_target_pairs={{0,2},{2,4},{4,6},{6,8},{8,10},{10,12},{12,14},{1,3},{3,5},{5,7},{... | collective-permute-start | bytes 393224 | tf_op jit(solution)/shard_map/ppermute | solution.py:21
  13.9 4.3 %collective-permute-start.3 = (f32[2,4,1,256]{3,2,1,0:T(1,128)S(1)}, f32[2,4,1,256]{3,2,1,0:T(1,128)S(1)}, u32[]{:S(2)}, u32[]{:S(2)}) collective-permute-start(f32[2,4,1,256]{3,2,1,0:T(1,128)S(1)} %get-tuple-element.55), channel_id=1, source_target_pairs={{1,0},{3,2},{5,4},{7,6},{9,8},{11,10},{13,12},{15,14},{17,16},{19,... | collective-permute-start | bytes 24584 | tf_op jit(solution)/shard_map/ppermute | solution.py:23
  15.2 3.8 collective-permute-start.2
  19.1 1.6 copy-start
  22.1 28.1 %collective-permute-start.4 = (f32[16,1,64,256]{3,0,2,1:T(8,128)S(1)}, f32[16,1,64,256]{3,0,2,1:T(8,128)S(1)}, u32[]{:S(2)}, u32[]{:S(2)}) collective-permute-start(f32[16,1,64,256]{3,0,2,1:T(8,128)S(1)} %get-tuple-element.45), channel_id=1, source_target_pairs={{2,0},{4,2},{6,4},{8,6},{10,8},{12,10},{14,12},{3,1},{5,3},{7,5},{... | collective-permute-start | bytes 3145736 | tf_op jit(solution)/shard_map/ppermute | solution.py:23
  23.4 49.4 %collective-permute-start.5 = (f32[16,1,64,256]{3,0,2,1:T(8,128)S(1)}, f32[16,1,64,256]{3,0,2,1:T(8,128)S(1)}, u32[]{:S(2)}, u32[]{:S(2)}) collective-permute-start(f32[16,1,64,256]{3,0,2,1:T(8,128)S(1)} %get-tuple-element.44), channel_id=1, source_target_pairs={{0,2},{2,4},{4,6},{6,8},{8,10},{10,12},{12,14},{1,3},{3,5},{5,7},{... | collective-permute-start | bytes 3145736 | tf_op jit(solution)/shard_map/ppermute | solution.py:21
  72.8 6.2 %collective-permute-start.7 = (f32[16,4,1,256]{3,0,2,1:T(8,128)S(1)}, f32[16,4,1,256]{3,0,2,1:T(8,128)S(1)}, u32[]{:S(2)}, u32[]{:S(2)}) collective-permute-start(f32[16,4,1,256]{3,0,2,1:T(8,128)S(1)} %get-tuple-element.33), channel_id=1, source_target_pairs={{0,1},{2,3},{4,5},{6,7},{8,9},{10,11},{12,13},{14,15},{16,17},{18,... | collective-permute-start | bytes 196616 | tf_op jit(solution)/shard_map/ppermute | solution.py:21
  74.7 4.3 %collective-permute-start.6 = (f32[16,4,1,256]{3,0,2,1:T(8,128)S(1)}, f32[16,4,1,256]{3,0,2,1:T(8,128)S(1)}, u32[]{:S(2)}, u32[]{:S(2)}) collective-permute-start(f32[16,4,1,256]{3,0,2,1:T(8,128)S(1)} %get-tuple-element.32), channel_id=1, source_target_pairs={{1,0},{3,2},{5,4},{7,6},{9,8},{11,10},{13,12},{15,14},{17,16},{19,... | collective-permute-start | bytes 196616 | tf_op jit(solution)/shard_map/ppermute | solution.py:23
  151.2 27.3 %collective-permute-start.8 = (f32[16,1,64,256]{3,0,2,1:T(8,128)S(1)}, f32[16,1,64,256]{3,0,2,1:T(8,128)S(1)}, u32[]{:S(2)}, u32[]{:S(2)}) collective-permute-start(f32[16,1,64,256]{3,0,2,1:T(8,128)S(1)} %get-tuple-element.41), channel_id=1, source_target_pairs={{2,0},{4,2},{6,4},{8,6},{10,8},{12,10},{14,12},{3,1},{5,3},{7,5},{... | collective-permute-start | bytes 3145736 | tf_op jit(solution)/shard_map/ppermute | solution.py:23
  152.5 44.5 %collective-permute-start.9 = (f32[16,1,64,256]{3,0,2,1:T(8,128)S(1)}, f32[16,1,64,256]{3,0,2,1:T(8,128)S(1)}, u32[]{:S(2)}, u32[]{:S(2)}) collective-permute-start(f32[16,1,64,256]{3,0,2,1:T(8,128)S(1)} %get-tuple-element.40), channel_id=1, source_target_pairs={{0,2},{2,4},{4,6},{6,8},{8,10},{10,12},{12,14},{1,3},{3,5},{5,7},{... | collective-permute-start | bytes 3145736 | tf_op jit(solution)/shard_map/ppermute | solution.py:21
  197.0 9.1 %collective-permute-start.11 = (f32[16,4,1,256]{3,0,2,1:T(8,128)S(1)}, f32[16,4,1,256]{3,0,2,1:T(8,128)S(1)}, u32[]{:S(2)}, u32[]{:S(2)}) collective-permute-start(f32[16,4,1,256]{3,0,2,1:T(8,128)S(1)} %get-tuple-element.31), channel_id=1, source_target_pairs={{0,1},{2,3},{4,5},{6,7},{8,9},{10,11},{12,13},{14,15},{16,17},{18,... | collective-permute-start | bytes 196616 | tf_op jit(solution)/shard_map/ppermute | solution.py:21
  199.0 7.2 %collective-permute-start.10 = (f32[16,4,1,256]{3,0,2,1:T(8,128)S(1)}, f32[16,4,1,256]{3,0,2,1:T(8,128)S(1)}, u32[]{:S(2)}, u32[]{:S(2)}) collective-permute-start(f32[16,4,1,256]{3,0,2,1:T(8,128)S(1)} %get-tuple-element.30), channel_id=1, source_target_pairs={{1,0},{3,2},{5,4},{7,6},{9,8},{11,10},{13,12},{15,14},{17,16},{19,... | collective-permute-start | bytes 196616 | tf_op jit(solution)/shard_map/ppermute | solution.py:23
  279.7 6.2 %copy-start.2 = (f32[2,8,128,256]{3,2,1,0:T(8,128)S(1)}, f32[2,8,128,256]{3,2,1,0:T(8,128)}, u32[]{:S(2)}) copy-start(f32[2,8,128,256]{3,2,1,0:T(8,128)} %copy.97) | copy-start | bytes 6291460
  279.9 27.4 %collective-permute-start.12 = (f32[16,1,64,256]{3,0,2,1:T(8,128)S(1)}, f32[16,1,64,256]{3,0,2,1:T(8,128)S(1)}, u32[]{:S(2)}, u32[]{:S(2)}) collective-permute-start(f32[16,1,64,256]{3,0,2,1:T(8,128)S(1)} %get-tuple-element.37), channel_id=1, source_target_pairs={{2,0},{4,2},{6,4},{8,6},{10,8},{12,10},{14,12},{3,1},{5,3},{7,5},{... | collective-permute-start | bytes 3145736 | tf_op jit(solution)/shard_map/ppermute | solution.py:23
  281.3 44.5 %collective-permute-start.13 = (f32[16,1,64,256]{3,0,2,1:T(8,128)S(1)}, f32[16,1,64,256]{3,0,2,1:T(8,128)S(1)}, u32[]{:S(2)}, u32[]{:S(2)}) collective-permute-start(f32[16,1,64,256]{3,0,2,1:T(8,128)S(1)} %get-tuple-element.36), channel_id=1, source_target_pairs={{0,2},{2,4},{4,6},{6,8},{8,10},{10,12},{12,14},{1,3},{3,5},{5,7},{... | collective-permute-start | bytes 3145736 | tf_op jit(solution)/shard_map/ppermute | solution.py:21
  290.9 38.2 %copy-start.1 = (f32[16,2,64,256]{3,0,2,1:T(8,128)S(1)}, f32[16,2,64,256]{3,0,2,1:T(8,128)}, u32[]{:S(2)}) copy-start(f32[16,2,64,256]{3,0,2,1:T(8,128)} %fusion.68) | copy-start | bytes 6291460
  325.8 8.5 %collective-permute-start.15 = (f32[16,4,1,256]{3,0,2,1:T(8,128)S(1)}, f32[16,4,1,256]{3,0,2,1:T(8,128)S(1)}, u32[]{:S(2)}, u32[]{:S(2)}) collective-permute-start(f32[16,4,1,256]{3,0,2,1:T(8,128)S(1)} %get-tuple-element.29), channel_id=1, source_target_pairs={{0,1},{2,3},{4,5},{6,7},{8,9},{10,11},{12,13},{14,15},{16,17},{18,... | collective-permute-start | bytes 196616 | tf_op jit(solution)/shard_map/ppermute | solution.py:21
  327.8 6.6 %collective-permute-start.14 = (f32[16,4,1,256]{3,0,2,1:T(8,128)S(1)}, f32[16,4,1,256]{3,0,2,1:T(8,128)S(1)}, u32[]{:S(2)}, u32[]{:S(2)}) collective-permute-start(f32[16,4,1,256]{3,0,2,1:T(8,128)S(1)} %get-tuple-element.28), channel_id=1, source_target_pairs={{1,0},{3,2},{5,4},{7,6},{9,8},{11,10},{13,12},{15,14},{17,16},{19,... | collective-permute-start | bytes 196616 | tf_op jit(solution)/shard_map/ppermute | solution.py:23
  337.6 1.3 copy-start.4
  385.1 4.6 %copy-start.3 = (f32[2,8,128,256]{3,2,1,0:T(8,128)S(1)}, f32[2,8,128,256]{3,2,1,0:T(8,128)}, u32[]{:S(2)}) copy-start(f32[2,8,128,256]{3,2,1,0:T(8,128)} %copy.93) | copy-start | bytes 6291460
  385.1 4.6 %copy-start.6 = (f32[16,2,64,256]{3,0,2,1:T(8,128)S(1)}, f32[16,2,64,256]{3,0,2,1:T(8,128)}, u32[]{:S(2)}) copy-start(f32[16,2,64,256]{3,0,2,1:T(8,128)} %fusion.52) | copy-start | bytes 6291460
  395.4 2.5 copy-start.5
